TPU v7x, 256 devices: a whole 4x4x8 slice. The times are simulated.
256 devices in a mesh: worker: 16 (over x, z_hi, core), fsdp: 16 (over z_lo, y).
Axes of the slice: x: 4, y: 4, z: 8 (z_hi: 2, z_lo: 4; z = z_hi * 4 + z_lo), core: 2. Of those that a mesh axis runs over, the one named last changes fastest.
Arguments:
- inputs: bfloat16 [16, 4096, 8192], P('worker', 'fsdp'), may hold values from -6 to 6
- output_grads: bfloat16 [16, 4096, 1024], P('worker', 'fsdp'), may hold values from -0.25 to 0.25
- local_params: float32 [16, 8192, 1024], P('worker', 'fsdp'), may hold values from -6 to 6
- first_moment: float32 [16, 8192, 1024], P('worker', 'fsdp'), may hold values from -4 to 4
- second_moment: float32 [16, 8192, 1024], P('worker', 'fsdp'), may hold values from 0.01 to 0.1
- global_params: float32 [8192, 1024], P(('fsdp', 'worker')), may hold values from -6 to 6
- momentum: float32 [8192, 1024], P(('fsdp', 'worker')), may hold values from -6 to 6
Outputs:
- new_params: float32 [8192, 1024], P('fsdp')
- new_momentum: float32 [8192, 1024], P(('fsdp', 'worker'))
All inputs are finite; a program needn't handle non-finite values.
Results may differ from a plain program's by a relative error of at most 0.0015.
Values may be sent and summed in bfloat16 or wider, within the bound.
A program may use at most 128 MiB of HBM per device.

v0:
```python
import jax
import jax.numpy as jnp
from jax import lax
from jax.sharding import PartitionSpec as P

beta_first = 0.8
beta_second = 0.9
inner_rate = 0.15
weight_decay = 0.1
adam_epsilon = 1e-08
outer_rate = 0.7
momentum_coef = 0.9
inner_count = 50


def shards(
    inputs, output_grads, local_params, first_moment, second_moment, global_params, momentum
):
    features = inputs[0]
    cotangents = output_grads[0]
    params = local_params[0]
    gradient = lax.psum_scatter(
        lax.dot_general(
            features, cotangents, (((0,), (0,)), ((), ())), preferred_element_type=jnp.float32
        ).astype(jnp.bfloat16),
        "fsdp",
        scatter_dimension=0,
        tiled=True,
    ).astype(jnp.float32)
    moment_one = beta_first * first_moment[0] + (1.0 - beta_first) * gradient
    moment_two = beta_second * second_moment[0] + (1.0 - beta_second) * gradient * gradient
    first_correction = 1.0 - beta_first**inner_count
    second_correction = 1.0 - beta_second**inner_count
    ratio = (
        moment_one / first_correction / (jnp.sqrt(moment_two / second_correction) + adam_epsilon)
    )
    stepped = params - inner_rate * (ratio + weight_decay * params)
    replicas = lax.axis_size("worker")
    anchor, moment_rows = (
        lax.all_gather(global_params, "worker", axis=0, tiled=True),
        lax.all_gather(momentum, "worker", axis=0, tiled=True),
    )
    pseudo_grad = anchor - stepped
    outer_grad = lax.psum(pseudo_grad, "worker") / replicas
    moment_full = momentum_coef * moment_rows + outer_grad
    fresh_rows = anchor - outer_rate * (outer_grad + momentum_coef * moment_full)
    share_rows = global_params.shape[0]
    worker_index = lax.axis_index("worker")
    own_moment = lax.dynamic_slice_in_dim(moment_full, worker_index * share_rows, share_rows, 0)
    return (fresh_rows, own_moment)


def solution(mesh):
    return jax.shard_map(
        shards,
        mesh=mesh,
        in_specs=(
            P("worker", "fsdp", None),
            P("worker", "fsdp", None),
            P("worker", "fsdp", None),
            P("worker", "fsdp", None),
            P("worker", "fsdp", None),
            P(("fsdp", "worker"), None),
            P(("fsdp", "worker"), None),
        ),
        out_specs=(P("fsdp", None), P(("fsdp", "worker"), None)),
        check_vma=False,
    )
```

profile of v0, /device:TPU:24, one launch (start us, length us, event | category | flops | bytes accessed | tf_op | source)
XLA Modules:
  0.0 505.8 jit_solution(11412425260126326226)
XLA Ops:
  8.0 0.0 copy-start
  8.0 0.0 all-gather.3.cloned.1.call-start
  8.1 0.7 all-gather.3.cloned.1.call-update
  8.7 0.0 reduce-scatter.2.cloned.1.call-start
  8.8 0.2 copy-done
  9.0 10.5 %convolution_convert_fusion = bf16[8192,1024]{1,0:T(8,128)(2,1)} fusion(bf16[1,256,8192]{2,1,0:T(8,128)(2,1)} %param.7, bf16[1,256,1024]{2,1,0:T(8,128)(2,1)S(1)} %copy-done), kind=kOutput, calls=%fused_computation | convolution fusion | flops 4303355904 | bytes 21495808 | tf_op jit(solution)/shard_map/dot_general | solution.py:23
  19.5 0.0 copy-start.2
  19.5 0.0 reduce-scatter.2.cloned.1.call-update
  19.5 0.0 all-gather.5.cloned.1.call-start
  19.6 0.7 all-gather.5.cloned.1.call-update
  20.3 0.0 all-reduce.2.cloned.1.call-start
  20.3 65.4 %all-gather.3.cloned.1.call-done = f32[512,1024]{1,0:T(8,128)} async-done(((f32[32,1024]{1,0:T(8,128)}), f32[512,1024]{1,0:T(8,128)}) %all-gather.3.cloned.1.call-update) | async-done | bytes 2097168 | tf_op jit(solution)/shard_map/all_gather | solution.py:40
  85.7 130.7 %reduce-scatter.2.cloned.1.call-done = bf16[512,1024]{1,0:T(8,128)(2,1)} async-done(((bf16[8192,1024]{1,0:T(8,128)(2,1)}), bf16[512,1024]{1,0:T(8,128)(2,1)}) %reduce-scatter.2.cloned.1.call-update) | async-done | bytes 1048592 | tf_op jit(solution)/shard_map/reduce_scatter | solution.py:22
  216.4 0.0 copy-done.2
  216.4 6.2 %fusion.7 = f32[512,1024]{1,0:T(8,128)} fusion(f32[512,1024]{1,0:T(8,128)} %all-gather.3.cloned.1.call-done, bf16[512,1024]{1,0:T(8,128)(2,1)} %reduce-scatter.2.cloned.1.call-done, f32[1,512,1024]{2,1,0:T(8,128)S(1)} %copy-done.2, f32[1,512,1024]{2,1,0:T(8,128)} %param.11, f32[1,512,1024]{2,1,0:T(8,128)} %param.10), kind=kLoop, calls=%fused_computation.10 | loop fusion | flops 8912896 | bytes 11534336 | tf_op jit(solution)/shard_map/sub | solution.py:43
  222.6 0.0 copy-start.1
  222.7 0.0 all-reduce.2.cloned.1.call-update
  222.7 68.5 %all-gather.5.cloned.1.call-done = f32[512,1024]{1,0:T(8,128)} async-done(((f32[32,1024]{1,0:T(8,128)}), f32[512,1024]{1,0:T(8,128)}) %all-gather.5.cloned.1.call-update) | async-done | bytes 2097168 | tf_op jit(solution)/shard_map/all_gather | solution.py:41
  291.2 202.5 %all-reduce.2.cloned.1.call-done = f32[512,1024]{1,0:T(8,128)} async-done(((f32[512,1024]{1,0:T(8,128)}), f32[512,1024]{1,0:T(8,128)}) %all-reduce.2.cloned.1.call-update) | async-done | bytes 2097168 | tf_op jit(solution)/shard_map/psum | solution.py:44
  493.7 0.0 copy-done.1
  493.7 4.3 multiply_add_fusion
  498.0 0.7 constant_dynamic-slice_fusion
Async XLA Ops:
  8.0 1.0 copy-start
  8.0 77.7 %all-gather.3.cloned.1.call-start = ((), (), s32[]{:S(2)}) async-start(), calls=%async_computation.1 | async-start | bytes 2228224 | tf_op jit(solution)/shard_map/all_gather | solution.py:40
  8.7 207.7 %reduce-scatter.2.cloned.1.call-start = ((), (), s32[]{:S(2)}) async-start(), calls=%async_computation.2 | async-start | bytes 17825792 | tf_op jit(solution)/shard_map/reduce_scatter | solution.py:22
  19.5 196.9 %copy-start.2 = (f32[1,512,1024]{2,1,0:T(8,128)S(1)}, f32[1,512,1024]{2,1,0:T(8,128)}, u32[]{:S(2)}) copy-start(f32[1,512,1024]{2,1,0:T(8,128)} %param.9) | copy-start | bytes 6291460
  19.5 271.6 %all-gather.5.cloned.1.call-start = ((), (), s32[]{:S(2)}) async-start(), calls=%async_computation.4 | async-start | bytes 2228224 | tf_op jit(solution)/shard_map/all_gather | solution.py:41
  20.3 473.4 %all-reduce.2.cloned.1.call-start = ((), (), s32[]{:S(2)}) async-start(), calls=%async_computation.3 | async-start | bytes 4194304 | tf_op jit(solution)/shard_map/psum | solution.py:44
  222.6 271.1 %copy-start.1 = (f32[512,1024]{1,0:T(8,128)S(1)}, f32[512,1024]{1,0:T(8,128)}, u32[]{:S(2)}) copy-start(f32[512,1024]{1,0:T(8,128)} %all-gather.3.cloned.1.call-done) | copy-start | bytes 6291460
Sparse Core Ops, SparseCore 0:
  11.5 74.1 all-gather.2
  88.4 202.7 all-gather.4
  294.4 199.2 all-reduce.1
Sparse Core Ops, SparseCore 1:
  19.6 196.8 reduce-scatter.1
where the time goes:
time: 506 us
  waiting for transfers between devices  469 us (93%)
  between operations  15.2 us (3%)
  matrix products  10.5 us (2%)
  other arithmetic  10.5 us (2%)
    psum x1, waiting for transfers between devices, shards(): outer_grad = lax.psum(pseudo_grad, 'worker') / replicas  203 us
    reduce_scatter x1, waiting for transfers between devices, shards(): lax.psum_scatter(lax.dot_general(features, cotangents, (((0,), (0,)), (()...  131 us
    all_gather x1, waiting for transfers between devices, shards(): lax.all_gather(momentum, 'worker', axis=0, tiled=True)  68.5 us
    all_gather x1, waiting for transfers between devices, shards(): lax.all_gather(global_params, 'worker', axis=0, tiled=True)  65.4 us
    dot_general x1, matrix products, shards(): lax.dot_general(features, cotangents, (((0,), (0,)), ((), ())), preferred...  10.5 us
  transfers between devices with their start and end apart: 4, of which 4 were waited for; matrix products, arithmetic and copies ran while one was open for 3% of the time, Pallas kernels for 0%

commit v1 on v0

--- a/solution.py
+++ b/solution.py
@@ -41,7 +41,8 @@
         lax.all_gather(momentum, "worker", axis=0, tiled=True),
     )
     pseudo_grad = anchor - stepped
-    outer_grad = lax.psum(pseudo_grad, "worker") / replicas
+    rounds_find = lambda work_x: jax.lax.all_gather(work_x, axis_name="worker").sum(axis=0)
+    outer_grad = rounds_find(pseudo_grad) / replicas
     moment_full = momentum_coef * moment_rows + outer_grad
     fresh_rows = anchor - outer_rate * (outer_grad + momentum_coef * moment_full)
     share_rows = global_params.shape[0]

time: 506 us -> 615 us (1.22)
  waiting for transfers between devices: 469 us -> 564 us
  other arithmetic: 10.5 us -> 22.7 us
    all_gather x0 -> x1, waiting for transfers between devices: none -> 318 us  [shards(): jax.lax.all_gather(work_x, axis_name='worker').sum(axis=0)]
    psum x1 -> x0, waiting for transfers between devices: 203 us -> none  [shards(): outer_grad = lax.psum(pseudo_grad, 'worker') / replicas]
    all_gather x1, waiting for transfers between devices: 68.5 us -> 47.8 us  [shards(): lax.all_gather(momentum, 'worker', axis=0, tiled=True)]
    reduce_sum x0 -> x1, other arithmetic: none -> 12.1 us  [shards(): jax.lax.all_gather(work_x, axis_name='worker').sum(axis=0)]
  transfers between devices with their start and end apart: 4 -> 4, of which waited for: 4 -> 4; matrix products, arithmetic and copies ran while one was open for 3% -> 4% of each run, Pallas kernels for 0% -> 0%
where the time goes in v1:
time: 615 us; the launch traced here: 613 us
  waiting for transfers between devices  564 us (92%)
  other arithmetic  22.7 us (4%)
  between operations  15.2 us (2%)
  matrix products  10.5 us (2%)
    all_gather x1, waiting for transfers between devices, shards(): jax.lax.all_gather(work_x, axis_name='worker').sum(axis=0)  318 us
    reduce_scatter x1, waiting for transfers between devices, shards(): lax.psum_scatter(lax.dot_general(features, cotangents, (((0,), (0,)), (()...  131 us
    all_gather x1, waiting for transfers between devices, shards(): lax.all_gather(global_params, 'worker', axis=0, tiled=True)  66.1 us
    all_gather x1, waiting for transfers between devices, shards(): lax.all_gather(momentum, 'worker', axis=0, tiled=True)  47.8 us
  transfers between devices with their start and end apart: 4, of which 4 were waited for; matrix products, arithmetic and copies ran while one was open for 4% of the time, Pallas kernels for 0%

profile of v1, /device:TPU:24, one launch (start us, length us, event | category | flops | bytes accessed | tf_op | source)
XLA Modules:
  0.0 613.0 jit_solution(11072957836683714489)
XLA Ops:
  8.0 0.0 copy-start
  8.0 0.0 all-gather.5.cloned.1.call-start
  8.1 0.7 all-gather.5.cloned.1.call-update
  8.7 0.0 reduce-scatter.2.cloned.1.call-start
  8.8 0.2 copy-done
  9.0 10.5 %convolution_convert_fusion = bf16[8192,1024]{1,0:T(8,128)(2,1)} fusion(bf16[1,256,8192]{2,1,0:T(8,128)(2,1)} %param.7, bf16[1,256,1024]{2,1,0:T(8,128)(2,1)S(1)} %copy-done), kind=kOutput, calls=%fused_computation | convolution fusion | flops 4303355904 | bytes 21495808 | tf_op jit(solution)/shard_map/dot_general | solution.py:23
  19.5 0.0 copy-start.2
  19.5 0.0 reduce-scatter.2.cloned.1.call-update
  19.5 0.0 all-gather.9.cloned.1.call-start
  19.6 66.1 %all-gather.5.cloned.1.call-done = f32[512,1024]{1,0:T(8,128)} async-done(((f32[32,1024]{1,0:T(8,128)}), f32[512,1024]{1,0:T(8,128)}) %all-gather.5.cloned.1.call-update) | async-done | bytes 2097168 | tf_op jit(solution)/shard_map/all_gather | solution.py:40
  85.7 130.7 %reduce-scatter.2.cloned.1.call-done = bf16[512,1024]{1,0:T(8,128)(2,1)} async-done(((bf16[8192,1024]{1,0:T(8,128)(2,1)}), bf16[512,1024]{1,0:T(8,128)(2,1)}) %reduce-scatter.2.cloned.1.call-update) | async-done | bytes 1048592 | tf_op jit(solution)/shard_map/reduce_scatter | solution.py:22
  216.4 0.0 copy-done.2
  216.4 6.2 %fusion.7 = f32[512,1024]{1,0:T(8,128)} fusion(f32[512,1024]{1,0:T(8,128)} %all-gather.5.cloned.1.call-done, bf16[512,1024]{1,0:T(8,128)(2,1)} %reduce-scatter.2.cloned.1.call-done, f32[1,512,1024]{2,1,0:T(8,128)S(1)} %copy-done.2, f32[1,512,1024]{2,1,0:T(8,128)} %param.11, f32[1,512,1024]{2,1,0:T(8,128)} %param.10), kind=kLoop, calls=%fused_computation.10 | loop fusion | flops 8912896 | bytes 11534336 | tf_op jit(solution)/shard_map/sub | solution.py:43
  222.7 0.0 all-gather.9.cloned.1.call-update
  222.7 0.0 all-gather.7.cloned.1.call-start
  222.7 0.7 all-gather.7.cloned.1.call-update
  223.4 317.5 %all-gather.9.cloned.1.call-done = f32[8192,1024]{1,0:T(8,128)} async-done(((f32[512,1024]{1,0:T(8,128)}), f32[8192,1024]{1,0:T(8,128)}) %all-gather.9.cloned.1.call-update) | async-done | bytes 33554448 | tf_op jit(solution)/shard_map/all_gather | solution.py:44
  541.0 12.1 %reduce_sum.9 = f32[512,1024]{1,0:T(8,128)S(1)} reduce(f32[16,512,1024]{2,1,0:T(8,128)} %bitcast.16, f32[]{:T(128)} %constant.13.clone.1), dimensions={0}, to_apply=%region_1.0 | reduce | flops 7864320 | bytes 35651588 | tf_op jit(solution)/shard_map/reduce_sum | solution.py:44
  553.1 47.8 %all-gather.7.cloned.1.call-done = f32[512,1024]{1,0:T(8,128)} async-done(((f32[32,1024]{1,0:T(8,128)}), f32[512,1024]{1,0:T(8,128)}) %all-gather.7.cloned.1.call-update) | async-done | bytes 2097168 | tf_op jit(solution)/shard_map/all_gather | solution.py:41
  600.9 0.0 copy-start.1
  600.9 4.4 multiply_add_fusion
  605.2 0.7 constant_dynamic-slice_fusion
  605.9 0.0 copy-done.1
Async XLA Ops:
  8.0 1.1 copy-start
  8.0 77.7 %all-gather.5.cloned.1.call-start = ((), (), s32[]{:S(2)}) async-start(), calls=%async_computation.1 | async-start | bytes 2228224 | tf_op jit(solution)/shard_map/all_gather | solution.py:40
  8.7 207.7 %reduce-scatter.2.cloned.1.call-start = ((), (), s32[]{:S(2)}) async-start(), calls=%async_computation.2 | async-start | bytes 17825792 | tf_op jit(solution)/shard_map/reduce_scatter | solution.py:22
  19.5 196.9 %copy-start.2 = (f32[1,512,1024]{2,1,0:T(8,128)S(1)}, f32[1,512,1024]{2,1,0:T(8,128)}, u32[]{:S(2)}) copy-start(f32[1,512,1024]{2,1,0:T(8,128)} %param.9) | copy-start | bytes 6291460
  19.5 521.4 %all-gather.9.cloned.1.call-start = ((), (), s32[]{:S(2)}) async-start(), calls=%async_computation.4 | async-start | bytes 35651584 | tf_op jit(solution)/shard_map/all_gather | solution.py:44
  222.7 378.2 %all-gather.7.cloned.1.call-start = ((), (), s32[]{:S(2)}) async-start(), calls=%async_computation.3 | async-start | bytes 2228224 | tf_op jit(solution)/shard_map/all_gather | solution.py:41
  600.9 5.0 copy-start.1
Sparse Core Ops, SparseCore 0:
  11.5 74.1 all-gather.4
  222.8 318.1 all-gather.8
  543.7 57.1 all-gather.6
Sparse Core Ops, SparseCore 1:
  19.6 196.8 reduce-scatter.1

commit v2 on v0

--- a/solution.py
+++ b/solution.py
@@ -36,8 +36,17 @@
     )
     stepped = params - inner_rate * (ratio + weight_decay * params)
     replicas = lax.axis_size("worker")
+    follow_frame = lambda local_block, bus_axis, at_axis: jnp.concatenate(
+        lax.all_to_all(
+            jnp.stack([local_block for _ in range(lax.psum(1, axis_name=bus_axis))]),
+            axis_name=bus_axis,
+            split_axis=0,
+            concat_axis=0,
+        ),
+        axis=at_axis,
+    )
     anchor, moment_rows = (
-        lax.all_gather(global_params, "worker", axis=0, tiled=True),
+        follow_frame(global_params, "worker", 0),
         lax.all_gather(momentum, "worker", axis=0, tiled=True),
     )
     pseudo_grad = anchor - stepped

time: 506 us -> 487 us (0.962)
  waiting for transfers between devices: 469 us -> 434 us
  starting transfers between devices: 0.16 us -> 11.2 us
    all_to_all x0 -> x1, waiting for transfers between devices: none -> 76.6 us  [shards(): lax.all_to_all(jnp.stack([local_block for _ in range(lax.psum(1, axis_nam...]
    all_gather x1, waiting for transfers between devices: 68.5 us -> 0.03 us  [shards(): lax.all_gather(momentum, 'worker', axis=0, tiled=True)]
    all_gather x1 -> x0, waiting for transfers between devices: 65.4 us -> none  [shards(): lax.all_gather(global_params, 'worker', axis=0, tiled=True)]
    reduce_scatter x1, waiting for transfers between devices: 131 us -> 154 us  [shards(): lax.psum_scatter(lax.dot_general(features, cotangents, (((0,), (0,)), (()...]
    all_to_all x0 -> x1, starting transfers between devices: none -> 11 us  [shards(): lax.all_to_all(jnp.stack([local_block for _ in range(lax.psum(1, axis_nam...]
  transfers between devices with their start and end apart: 4 -> 4, of which waited for: 4 -> 3; matrix products, arithmetic and copies ran while one was open for 3% -> 2% of each run, Pallas kernels for 0% -> 0%
where the time goes in v2:
time: 487 us; the launch traced here: 485 us
  waiting for transfers between devices  434 us (89%)
  between operations  15.5 us (3%)
  starting transfers between devices  11.2 us (2%)
  matrix products  10.5 us (2%)
  other arithmetic  10.5 us (2%)
    psum x1, waiting for transfers between devices, shards(): outer_grad = lax.psum(pseudo_grad, 'worker') / replicas  203 us
    reduce_scatter x1, waiting for transfers between devices, shards(): lax.psum_scatter(lax.dot_general(features, cotangents, (((0,), (0,)), (()...  154 us
    all_to_all x1, waiting for transfers between devices, shards(): lax.all_to_all(jnp.stack([local_block for _ in range(lax.psum(1, axis_nam...  76.6 us
    all_to_all x1, starting transfers between devices, shards(): lax.all_to_all(jnp.stack([local_block for _ in range(lax.psum(1, axis_nam...  11 us
    dot_general x1, matrix products, shards(): lax.dot_general(features, cotangents, (((0,), (0,)), ((), ())), preferred...  10.5 us
  transfers between devices with their start and end apart: 4, of which 3 were waited for; matrix products, arithmetic and copies ran while one was open for 2% of the time, Pallas kernels for 0%

profile of v2, /device:TPU:24, one launch (start us, length us, event | category | flops | bytes accessed | tf_op | source)
XLA Modules:
  0.0 485.4 jit_solution(7887383360606608684)
XLA Ops:
  8.0 0.0 copy-start
  8.0 0.0 reduce-scatter.2.cloned.1.call-start
  8.1 1.0 copy-done
  9.0 10.5 %convolution_convert_fusion = bf16[8192,1024]{1,0:T(8,128)(2,1)} fusion(bf16[1,256,8192]{2,1,0:T(8,128)(2,1)} %param.7, bf16[1,256,1024]{2,1,0:T(8,128)(2,1)S(1)} %copy-done), kind=kOutput, calls=%fused_computation | convolution fusion | flops 4303355904 | bytes 21495808 | tf_op jit(solution)/shard_map/dot_general | solution.py:23
  19.5 0.0 copy-start.1
  19.5 0.0 reduce-scatter.2.cloned.1.call-update
  19.5 0.9 copy-done.1
  20.4 1.6 stack.2
  22.0 11.0 %all-to-all-start = ((f32[16,32,1024]{2,1,0:T(8,128)}), f32[16,32,1024]{2,1,0:T(8,128)S(1)}, u32[]{:S(2)}, u32[]{:S(2)}) async-start(f32[16,32,1024]{2,1,0:T(8,128)} %stack.2), calls=%async_computation | async-start | bytes 4194304 | tf_op jit(solution)/shard_map/all_to_all | solution.py:40
  33.0 0.0 all-gather.2.cloned.1.call-start
  33.1 0.5 all-gather.2.cloned.1.call-update
  33.6 0.0 all-reduce.2.cloned.1.call-start
  33.7 76.6 %all-to-all-done = f32[16,32,1024]{2,1,0:T(8,128)S(1)} async-done(((f32[16,32,1024]{2,1,0:T(8,128)}), f32[16,32,1024]{2,1,0:T(8,128)S(1)}, u32[]{:S(2)}, u32[]{:S(2)}) %all-to-all-start) | async-done | bytes 2097184 | tf_op jit(solution)/shard_map/all_to_all | solution.py:40
  110.3 153.8 %reduce-scatter.2.cloned.1.call-done = bf16[512,1024]{1,0:T(8,128)(2,1)} async-done(((bf16[8192,1024]{1,0:T(8,128)(2,1)}), bf16[512,1024]{1,0:T(8,128)(2,1)}) %reduce-scatter.2.cloned.1.call-update) | async-done | bytes 1048592 | tf_op jit(solution)/shard_map/reduce_scatter | solution.py:22
  264.1 6.2 %fusion.7 = f32[512,1024]{1,0:T(8,128)} fusion(bf16[512,1024]{1,0:T(8,128)(2,1)} %reduce-scatter.2.cloned.1.call-done, f32[1,512,1024]{2,1,0:T(8,128)} %param.9, f32[16,32,1024]{2,1,0:T(8,128)S(1)} %all-to-all-done, f32[1,512,1024]{2,1,0:T(8,128)} %param.11, f32[1,512,1024]{2,1,0:T(8,128)} %param.10), kind=kLoop, calls=%fused_computation.10 | loop fusion | flops 8912896 | bytes 11534336 | tf_op jit(solution)/shard_map/sub | solution.py:52
  270.3 0.0 all-reduce.2.cloned.1.call-update
  270.3 0.0 all-gather.2.cloned.1.call-done
  270.4 202.6 %all-reduce.2.cloned.1.call-done = f32[512,1024]{1,0:T(8,128)} async-done(((f32[512,1024]{1,0:T(8,128)}), f32[512,1024]{1,0:T(8,128)}) %all-reduce.2.cloned.1.call-update) | async-done | bytes 2097168 | tf_op jit(solution)/shard_map/psum | solution.py:53
  472.9 4.3 multiply_add_fusion
  477.3 0.7 constant_dynamic-slice_fusion
Async XLA Ops:
  8.0 1.0 copy-start
  8.0 256.0 %reduce-scatter.2.cloned.1.call-start = ((), (), s32[]{:S(2)}) async-start(), calls=%async_computation.2 | async-start | bytes 17825792 | tf_op jit(solution)/shard_map/reduce_scatter | solution.py:22
  19.5 0.9 copy-start.1
  22.0 88.3 %all-to-all-start = ((f32[16,32,1024]{2,1,0:T(8,128)}), f32[16,32,1024]{2,1,0:T(8,128)S(1)}, u32[]{:S(2)}, u32[]{:S(2)}) async-start(f32[16,32,1024]{2,1,0:T(8,128)} %stack.2), calls=%async_computation | async-start | bytes 4194304 | tf_op jit(solution)/shard_map/all_to_all | solution.py:40
  33.0 237.3 %all-gather.2.cloned.1.call-start = ((), (), s32[]{:S(2)}) async-start(), calls=%async_computation.4 | async-start | bytes 2228224 | tf_op jit(solution)/shard_map/all_gather | solution.py:50
  33.6 439.3 %all-reduce.2.cloned.1.call-start = ((), (), s32[]{:S(2)}) async-start(), calls=%async_computation.3 | async-start | bytes 4194304 | tf_op jit(solution)/shard_map/psum | solution.py:53
Sparse Core Ops, SparseCore 0:
  19.7 244.3 reduce-scatter.1
Sparse Core Ops, SparseCore 1:
  36.2 105.1 all-gather.1
  270.4 202.5 all-reduce.1
